TPU v7x, 512 devices: a whole 4x8x8 slice. The times are simulated.
512 devices in a mesh: grow: 32 (over x_hi, y, core), gcol: 16 (over z, x_lo).
Axes of the slice: x: 4 (x_hi: 2, x_lo: 2; x = x_hi * 2 + x_lo), y: 8, z: 8, core: 2. Of those that a mesh axis runs over, the one named last changes fastest.
Arguments:
- coefficients: bfloat16 [20480, 49152], P('grow', 'gcol'), may hold values from -0.02734375 to 0.02734375
- tile_mask: int32 [160, 384], P('grow', 'gcol'), may hold values 0 or 1
- duals: float32 [20480], P('grow'), may hold values from -6 to 6
- costs: float32 [49152], P('gcol'), may hold values from -6 to 6
- primal: float32 [49152], P('gcol'), may hold values from 0.1 to 10
- fixed: int32 [49152], P('gcol'), may hold values 0 or 1
Outputs:
- normal_window: float32 [1024, 20480], P('gcol', 'grow')
- factor_window: float32 [1024, 20480], P('gcol', 'grow')
All inputs are finite; a program needn't handle non-finite values. No bound on the sum of `tile_mask` or of `fixed` on one device may be relied on, other than what follows from the above.
Results may differ from a plain program's by a relative error of at most 0.0023.
Values may be sent and summed in bfloat16 or wider, within the bound.
A program may use at most 64 MiB of HBM per device.

v0:
```python
import jax
import jax.numpy as jnp
from jax import lax
from jax.sharding import PartitionSpec as P

PANEL = 512
SOFTNESS = 0.25
DIAGONAL_SHIFT = 0.5


def split_normal(normal, blocks_own, panel_per, rows_dev):
    split = normal.reshape(blocks_own, 2, panel_per, rows_dev)
    own_panel = split[:, 0].reshape(blocks_own * panel_per, rows_dev)
    own_trailing = split[:, 1].reshape(blocks_own * panel_per, rows_dev)
    panel_all = lax.all_gather(own_panel, "gcol", axis=0, tiled=True)
    return (own_trailing, panel_all)


def shards(coefficients, tile_mask, duals, costs, primal, fixed):
    rows_dev, columns = coefficients.shape
    row_count = lax.axis_size("grow")
    col_count = lax.axis_size("gcol")
    panel_per = PANEL // row_count
    blocks_own = row_count // col_count
    local_win = blocks_own * 2 * panel_per
    tile_rows, tile_cols = tile_mask.shape
    side = rows_dev // tile_rows
    expanded = jnp.broadcast_to(
        tile_mask[:, None, :, None], (tile_rows, side, tile_cols, side)
    ).reshape(rows_dev, columns)
    masked = coefficients * expanded.astype(jnp.bfloat16)
    partial_products = jnp.dot(
        duals, masked, preferred_element_type=jnp.float32, precision=lax.Precision.HIGHEST
    )
    products = lax.psum(partial_products, "grow")
    reduced = costs - products
    scaling = (1 - fixed).astype(jnp.float32) * primal / jnp.sqrt(reduced * reduced + SOFTNESS)
    scaled = (masked * scaling[None, :]).astype(jnp.bfloat16)
    window_all = lax.all_gather(masked[: 2 * panel_per], "grow", axis=0, tiled=True)
    col_index = lax.axis_index("gcol")
    normal = lax.psum_scatter(
        lax.dot_general(
            window_all, scaled, (((1,), (1,)), ((), ())), preferred_element_type=jnp.float32
        ),
        "gcol",
        scatter_dimension=0,
        tiled=True,
    )
    own_trailing, panel_all = split_normal(normal, blocks_own, panel_per, rows_dev)
    corner = lax.all_gather(panel_all[:, :panel_per], "grow", axis=1, tiled=True)
    shifted = 0.5 * (corner + corner.T) + DIAGONAL_SHIFT * jnp.eye(PANEL, dtype=jnp.float32)
    lower = jnp.linalg.cholesky(shifted)
    factor_panel = jax.scipy.linalg.solve_triangular(lower, panel_all, lower=True)
    edge_all = lax.all_gather(
        factor_panel[:, panel_per : 2 * panel_per], "grow", axis=1, tiled=True
    )
    own_edge = lax.dynamic_slice_in_dim(
        edge_all, col_index * (blocks_own * panel_per), blocks_own * panel_per, 1
    )
    updated = own_trailing - jnp.dot(own_edge.T, factor_panel, precision=lax.Precision.HIGHEST)
    panel_rows = lax.dynamic_slice_in_dim(
        factor_panel, col_index * (blocks_own * panel_per), blocks_own * panel_per, 0
    )
    factor = jnp.stack(
        [
            panel_rows.reshape(blocks_own, panel_per, rows_dev),
            updated.reshape(blocks_own, panel_per, rows_dev),
        ],
        axis=1,
    )
    return (normal, factor.reshape(local_win, rows_dev))


def solution(mesh):
    placed = (P("grow", "gcol"), P("grow", "gcol"), P("grow"), P("gcol"), P("gcol"), P("gcol"))
    return jax.shard_map(
        shards,
        mesh=mesh,
        in_specs=placed,
        out_specs=(P("gcol", "grow"), P("gcol", "grow")),
        check_vma=False,
    )
```

profile of v0, /device:TPU:1, one launch (start us, length us, event | category | flops | bytes accessed | tf_op | source)
XLA Modules:
  0.0 642.4 jit_solution(5346488050266648543)
XLA Ops:
  9.9 1.9 copy-done
  12.6 3.7 fusion.38
  16.3 130.1 %psum.7 = f32[3072]{0:T(1024)S(1)} all-reduce(f32[3072]{0:T(1024)S(1)} %bitcast.77), channel_id=1, replica_groups=mesh['grow'=32,'gcol'=16] {'grow'}, use_global_device_ids=true, to_apply=%region_0.0 | all-reduce | flops 3072 | bytes 24576 | tf_op jit(solution)/shard_map/psum | solution.py:35
  146.5 9.5 %fusion = f32[1024,640]{1,0:T(8,128)} fusion(bf16[1024,3072]{1,0:T(8,128)(2,1)} %all-gather.5.cloned.1.call-done, bf16[640,3072]{1,0:T(8,128)(2,1)} %copy-done, f32[3072]{0:T(1024)S(1)} %rsqrt_multiply_fusion), kind=kOutput, calls=%fused_computation.3 | convolution fusion | flops 4032430080 | bytes 12857344 | tf_op jit(solution)/shard_map/dot_general | solution.py:42
  156.0 74.2 %reduce-scatter.2.cloned.1.call-done = f32[64,640]{1,0:T(8,128)} async-done(((f32[1024,640]{1,0:T(8,128)}), f32[64,640]{1,0:T(8,128)}) %reduce-scatter.2.cloned.1.call-update) | async-done | bytes 163856 | tf_op jit(solution)/shard_map/reduce_scatter | solution.py:41
  230.3 1.6 fusion.37
  231.9 71.6 %all-gather.7.cloned.1.call-done = f32[512,640]{1,0:T(8,128)} async-done(((f32[32,640]{1,0:T(8,128)}), f32[512,640]{1,0:T(8,128)}) %all-gather.7.cloned.1.call-update) | async-done | bytes 1310736 | tf_op jit(solution)/shard_map/all_gather | solution.py:15
  305.8 94.8 %all-gather.9.cloned.1.call-done = f32[512,512]{0,1:T(8,128)} async-done(((f32[512,16]{0,1:T(8,128)}), f32[512,512]{0,1:T(8,128)}) %all-gather.9.cloned.1.call-update) | async-done | bytes 1048592 | tf_op jit(solution)/shard_map/all_gather | solution.py:50
  400.6 1.6 copy.19
  403.1 11.7 %cholesky.103 = f32[128,128]{1,0:T(8,128)S(1)} custom-call(f32[128,128]{1,0:T(8,128)S(1)} %cholesky.263), custom_call_target="Cholesky" | custom-call | tf_op jit(solution)/shard_map/jit(cholesky)/cholesky | solution.py:52
  414.8 9.8 %custom-call.31 = f32[1,128,128]{1,2,0:T(8,128)S(1)} custom-call(f32[1,128,128]{2,1,0:T(8,128)S(1)} %get-tuple-element.31), custom_call_target="InvertDiagBlocksLowerTriangular" | custom-call | tf_op jit(solution)/shard_map/jit(cholesky)/cholesky | solution.py:52
  427.1 11.7 %cholesky.215 = f32[128,128]{1,0:T(8,128)S(1)} custom-call(f32[128,128]{1,0:T(8,128)S(1)} %cholesky.267), custom_call_target="Cholesky" | custom-call | tf_op jit(solution)/shard_map/jit(cholesky)/cholesky | solution.py:52
  438.8 9.9 %custom-call.32 = f32[1,128,128]{1,2,0:T(8,128)S(1)} custom-call(f32[1,128,128]{2,1,0:T(8,128)S(1)} %get-tuple-element.28), custom_call_target="InvertDiagBlocksLowerTriangular" | custom-call | tf_op jit(solution)/shard_map/jit(cholesky)/cholesky | solution.py:52
  450.9 13.2 %cholesky.236 = f32[128,128]{1,0:T(8,128)} custom-call(f32[128,128]{1,0:T(8,128)} %cholesky.272), custom_call_target="Cholesky" | custom-call | tf_op jit(solution)/shard_map/jit(cholesky)/cholesky | solution.py:52
  466.3 11.3 %custom-call.33 = f32[1,128,128]{1,2,0:T(8,128)} custom-call(f32[1,128,128]{2,1,0:T(8,128)} %get-tuple-element.25), custom_call_target="InvertDiagBlocksLowerTriangular" | custom-call | tf_op jit(solution)/shard_map/jit(cholesky)/cholesky | solution.py:52
  479.0 11.9 %cholesky.253 = f32[128,128]{1,0:T(8,128)S(1)} custom-call(f32[128,128]{1,0:T(8,128)S(1)} %convolution_subtract_fusion.6), custom_call_target="Cholesky" | custom-call | tf_op jit(solution)/shard_map/jit(cholesky)/cholesky | solution.py:52
  494.9 10.7 %while.1 = (s32[]{:T(128)}, f32[512,512]{1,0:T(8,128)S(1)}, s32[4,2]{0,1:T(2,128)S(1)}, f32[4,128,128]{2,1,0:T(8,128)}, s32[]{:T(128)}) while((s32[]{:T(128)}, f32[512,512]{1,0:T(8,128)S(1)}, s32[4,2]{0,1:T(2,128)S(1)}, f32[4,128,128]{2,1,0:T(8,128)}, s32[]{:T(128)}) %tuple.32), condition=%wide.while_cond, body=%wide.while_body.sunk | while | flops 2 | bytes 132705 | solution.py:53
  495.6 2.0 bitcast_dynamic-update-slice_fusion.2
  498.2 2.0 bitcast_dynamic-update-slice_fusion.2
  500.9 2.0 bitcast_dynamic-update-slice_fusion.2
  503.6 2.0 bitcast_dynamic-update-slice_fusion.2
  505.6 40.1 %custom-call.34 = f32[4,128,128]{1,2,0:T(8,128)S(1)} custom-call(f32[4,128,128]{2,1,0:T(8,128)} %get-tuple-element.9), custom_call_target="InvertDiagBlocksLowerTriangular" | custom-call | tf_op jit(solution)/shard_map/jit(_solve_triangular)/triangular_solve | solution.py:53
  553.2 80.1 %all-gather.11.cloned.1.call-done = f32[512,512]{0,1:T(8,128)} async-done(((f32[512,16]{0,1:T(8,128)}), f32[512,512]{0,1:T(8,128)}) %all-gather.11.cloned.1.call-update) | async-done | bytes 1048592 | tf_op jit(solution)/shard_map/all_gather | solution.py:54
  633.3 1.7 convolution_subtract_fusion.5
  (83 shorter events, 27.1 us)
Async XLA Ops:
  7.2 139.3 %all-gather.5.cloned.1.call-start = ((), (), s32[]{:S(2)}) async-start(), calls=%async_computation.1 | async-start | bytes 6488064 | tf_op jit(solution)/shard_map/all_gather | solution.py:39
  7.2 2.1 copy-start.2
  9.3 3.2 copy-start.9
  9.9 1.9 copy-start
  11.8 134.6 %copy-start.6 = (f32[3072]{0:T(1024)S(1)}, f32[3072]{0:T(1024)}, u32[]{:S(2)}) copy-start(f32[3072]{0:T(1024)} %param.9) | copy-start | bytes 36868
  11.8 134.6 %copy-start.7 = (f32[3072]{0:T(1024)S(1)}, f32[3072]{0:T(1024)}, u32[]{:S(2)}) copy-start(f32[3072]{0:T(1024)} %param.10) | copy-start | bytes 36868
  11.8 134.6 %copy-start.8 = (s32[3072]{0:T(1024)S(1)}, s32[3072]{0:T(1024)}, u32[]{:S(2)}) copy-start(s32[3072]{0:T(1024)} %param.11) | copy-start | bytes 36868
  12.5 217.7 %reduce-scatter.2.cloned.1.call-start = ((), (), s32[]{:S(2)}) async-start(), calls=%async_computation.2 | async-start | bytes 2785280 | tf_op jit(solution)/shard_map/reduce_scatter | solution.py:41
  156.0 147.6 %all-gather.7.cloned.1.call-start = ((), (), s32[]{:S(2)}) async-start(), calls=%async_computation.3 | async-start | bytes 1392640 | tf_op jit(solution)/shard_map/all_gather | solution.py:15
  231.9 168.7 %all-gather.9.cloned.1.call-start = ((), (), s32[]{:S(2)}) async-start(), calls=%async_computation.4 | async-start | bytes 1081344 | tf_op jit(solution)/shard_map/all_gather | solution.py:50
  305.3 328.0 %all-gather.11.cloned.1.call-start = ((), (), s32[]{:S(2)}) async-start(), calls=%async_computation.5 | async-start | bytes 1081344 | tf_op jit(solution)/shard_map/all_gather | solution.py:54
  400.6 1.7 copy-start.1
  426.1 119.6 %copy-start.3 = (f32[512,640]{1,0:T(8,128)S(1)}, f32[512,640]{1,0:T(8,128)}, u32[]{:S(2)}) copy-start(f32[512,640]{1,0:T(8,128)} %all-gather.7.cloned.1.call-done) | copy-start | bytes 3932164
  545.7 0.7 copy-start.4
  550.8 82.4 %copy-start.5 = (f32[2,1,16,640]{3,2,1,0:T(8,128)S(1)}, f32[2,1,16,640]{3,2,1,0:T(8,128)}, u32[]{:S(2)}) copy-start(f32[2,1,16,640]{3,2,1,0:T(8,128)} %get-tuple-element.21) | copy-start | bytes 245764
Sparse Core Ops, SparseCore 0:
  12.6 105.7 all-gather.4
  156.1 74.1 reduce-scatter.1
  232.9 70.5 all-gather.6
  307.3 93.2 all-gather.8
  553.3 79.9 all-gather.10
where the time goes:
time: 648 us; the launch traced here: 642 us
  waiting for transfers between devices  321 us (50%)
  blocking collectives  130 us (20%)
  other arithmetic  125 us (19%)
  matrix products  25.4 us (4%)
  local copies, waits for them, and re-layouts  23.3 us (4%)
  between operations  16.8 us (3%)
    psum x1, blocking collectives, shards(): products = lax.psum(partial_products, 'grow')  130 us
    all_gather x1, waiting for transfers between devices, shards(): lax.all_gather(panel_all[:, :panel_per], 'grow', axis=1, tiled=True)  94.8 us
    another operation x14, other arithmetic, shards(): lower = jnp.linalg.cholesky(shifted)  83.1 us
    all_gather x1, waiting for transfers between devices, shards(): lax.all_gather(factor_panel[:, panel_per:2 * panel_per], 'grow', axis=1,...  80.1 us
    reduce_scatter x1, waiting for transfers between devices, shards(): lax.psum_scatter(lax.dot_general(window_all, scaled, (((1,), (1,)), ((),...  74.2 us
    all_gather x1, waiting for transfers between devices, split_normal(): panel_all = lax.all_gather(own_panel, 'gcol', axis=0, tiled=True)  71.6 us
    another operation x4, other arithmetic, shards(): jax.scipy.linalg.solve_triangular(lower, panel_all, lower=True)  40.3 us
  transfers between devices with their start and end apart: 5, of which 4 were waited for; matrix products, arithmetic and copies ran while one was open for 1% of the time, Pallas kernels for 0%

commit v1 on v0

--- a/solution.py
+++ b/solution.py
@@ -8,11 +8,18 @@
 DIAGONAL_SHIFT = 0.5
 
 
+def exchange_gather(value, name, dim):
+    size = lax.axis_size(name)
+    blocks = jnp.stack([value for _ in range(size)])
+    blocks = lax.all_to_all(blocks, name, split_axis=0, concat_axis=0)
+    return jnp.concatenate(blocks, axis=dim)
+
+
 def split_normal(normal, blocks_own, panel_per, rows_dev):
     split = normal.reshape(blocks_own, 2, panel_per, rows_dev)
     own_panel = split[:, 0].reshape(blocks_own * panel_per, rows_dev)
     own_trailing = split[:, 1].reshape(blocks_own * panel_per, rows_dev)
-    panel_all = lax.all_gather(own_panel, "gcol", axis=0, tiled=True)
+    panel_all = exchange_gather(own_panel, "gcol", 0)
     return (own_trailing, panel_all)
 
 

time: 648 us -> 588 us (0.907)
  waiting for transfers between devices: 321 us -> 243 us
  blocking collectives: 130 us -> 158 us
    all_gather x1 -> x0, waiting for transfers between devices: 71.6 us -> none  [split_normal(): panel_all = lax.all_gather(own_panel, 'gcol', axis=0, tiled=True)]
    all_to_all x0 -> x1, blocking collectives: none -> 27.9 us  [exchange_gather(): blocks = lax.all_to_all(blocks, name, split_axis=0, concat_axis=0)]
    all_gather x1, waiting for transfers between devices: 94.8 us -> 88.3 us  [shards(): lax.all_gather(panel_all[:, :panel_per], 'grow', axis=1, tiled=True)]
  transfers between devices with their start and end apart: 5 -> 4, of which waited for: 4 -> 3; matrix products, arithmetic and copies ran while one was open for 1% -> 1% of each run, Pallas kernels for 0% -> 0%
where the time goes in v1:
time: 588 us; the launch traced here: 583 us
  waiting for transfers between devices  243 us (41%)
  blocking collectives  158 us (27%)
  other arithmetic  121 us (21%)
  matrix products  22.1 us (4%)
  local copies, waits for them, and re-layouts  20.8 us (4%)
  between operations  16.9 us (3%)
    psum x1, blocking collectives, shards(): products = lax.psum(partial_products, 'grow')  130 us
    all_gather x1, waiting for transfers between devices, shards(): lax.all_gather(panel_all[:, :panel_per], 'grow', axis=1, tiled=True)  88.3 us
    all_gather x1, waiting for transfers between devices, shards(): lax.all_gather(factor_panel[:, panel_per:2 * panel_per], 'grow', axis=1,...  80.1 us
    another operation x14, other arithmetic, shards(): lower = jnp.linalg.cholesky(shifted)  78.7 us
    reduce_scatter x1, waiting for transfers between devices, shards(): lax.psum_scatter(lax.dot_general(window_all, scaled, (((1,), (1,)), ((),...  74.2 us
    another operation x4, other arithmetic, shards(): jax.scipy.linalg.solve_triangular(lower, panel_all, lower=True)  40.9 us
    all_to_all x1, blocking collectives, exchange_gather(): blocks = lax.all_to_all(blocks, name, split_axis=0, concat_axis=0)  27.9 us
  transfers between devices with their start and end apart: 4, of which 3 were waited for; matrix products, arithmetic and copies ran while one was open for 1% of the time, Pallas kernels for 0%

profile of v1, /device:TPU:1, one launch (start us, length us, event | category | flops | bytes accessed | tf_op | source)
XLA Modules:
  0.0 582.6 jit_solution(14502172686337505011)
XLA Ops:
  9.9 1.9 copy-done
  12.6 3.7 fusion.38
  16.3 130.1 %psum.7 = f32[3072]{0:T(1024)S(1)} all-reduce(f32[3072]{0:T(1024)S(1)} %bitcast.86), channel_id=1, replica_groups=mesh['grow'=32,'gcol'=16] {'grow'}, use_global_device_ids=true, to_apply=%region_0.0 | all-reduce | flops 3072 | bytes 24576 | tf_op jit(solution)/shard_map/psum | solution.py:42
  146.5 9.5 %fusion = f32[1024,640]{1,0:T(8,128)} fusion(bf16[1024,3072]{1,0:T(8,128)(2,1)} %all-gather.4.cloned.1.call-done, bf16[640,3072]{1,0:T(8,128)(2,1)} %copy-done, f32[3072]{0:T(1024)S(1)} %rsqrt_multiply_fusion), kind=kOutput, calls=%fused_computation.3 | convolution fusion | flops 4032430080 | bytes 12857344 | tf_op jit(solution)/shard_map/dot_general | solution.py:49
  156.0 74.2 %reduce-scatter.2.cloned.1.call-done = f32[64,640]{1,0:T(8,128)} async-done(((f32[1024,640]{1,0:T(8,128)}), f32[64,640]{1,0:T(8,128)}) %reduce-scatter.2.cloned.1.call-update) | async-done | bytes 163856 | tf_op jit(solution)/shard_map/reduce_scatter | solution.py:48
  231.3 27.9 %all_to_all.5 = f32[16,32,640]{2,1,0:T(8,128)S(1)} all-to-all(f32[16,32,640]{2,1,0:T(8,128)S(1)} %stack.6), channel_id=1, replica_groups=mesh['grow'=32,'gcol'=16] {'gcol'}, dimensions={0} | all-to-all | bytes 2621440 | tf_op jit(solution)/shard_map/all_to_all | solution.py:14
  262.1 88.3 %all-gather.6.cloned.1.call-done = f32[512,512]{0,1:T(8,128)} async-done(((f32[512,16]{0,1:T(8,128)}), f32[512,512]{0,1:T(8,128)}) %all-gather.6.cloned.1.call-update) | async-done | bytes 1048592 | tf_op jit(solution)/shard_map/all_gather | solution.py:57
  350.4 1.6 copy.17
  352.9 11.7 %cholesky.103 = f32[128,128]{1,0:T(8,128)S(1)} custom-call(f32[128,128]{1,0:T(8,128)S(1)} %cholesky.263), custom_call_target="Cholesky" | custom-call | tf_op jit(solution)/shard_map/jit(cholesky)/cholesky | solution.py:59
  364.7 9.8 %custom-call.31 = f32[1,128,128]{1,2,0:T(8,128)S(1)} custom-call(f32[1,128,128]{2,1,0:T(8,128)S(1)} %get-tuple-element.35), custom_call_target="InvertDiagBlocksLowerTriangular" | custom-call | tf_op jit(solution)/shard_map/jit(cholesky)/cholesky | solution.py:59
  375.3 11.7 %cholesky.215 = f32[128,128]{1,0:T(8,128)S(1)} custom-call(f32[128,128]{1,0:T(8,128)S(1)} %cholesky.267), custom_call_target="Cholesky" | custom-call | tf_op jit(solution)/shard_map/jit(cholesky)/cholesky | solution.py:59
  387.0 10.0 %custom-call.32 = f32[1,128,128]{1,2,0:T(8,128)S(1)} custom-call(f32[1,128,128]{2,1,0:T(8,128)S(1)} %get-tuple-element.32), custom_call_target="InvertDiagBlocksLowerTriangular" | custom-call | tf_op jit(solution)/shard_map/jit(cholesky)/cholesky | solution.py:59
  397.7 11.7 %cholesky.236 = f32[128,128]{1,0:T(8,128)S(1)} custom-call(f32[128,128]{1,0:T(8,128)S(1)} %cholesky.272), custom_call_target="Cholesky" | custom-call | tf_op jit(solution)/shard_map/jit(cholesky)/cholesky | solution.py:59
  410.1 9.8 %custom-call.33 = f32[1,128,128]{1,2,0:T(8,128)S(1)} custom-call(f32[1,128,128]{2,1,0:T(8,128)S(1)} %get-tuple-element.29), custom_call_target="InvertDiagBlocksLowerTriangular" | custom-call | tf_op jit(solution)/shard_map/jit(cholesky)/cholesky | solution.py:59
  420.5 11.9 %cholesky.253 = f32[128,128]{1,0:T(8,128)S(1)} custom-call(f32[128,128]{1,0:T(8,128)S(1)} %convolution_subtract_fusion.6), custom_call_target="Cholesky" | custom-call | tf_op jit(solution)/shard_map/jit(cholesky)/cholesky | solution.py:59
  436.5 10.4 %while.1 = (s32[]{:T(128)}, f32[512,512]{1,0:T(8,128)S(1)}, s32[4,2]{0,1:T(2,128)S(1)}, f32[4,128,128]{2,1,0:T(8,128)}, s32[]{:T(128)}) while((s32[]{:T(128)}, f32[512,512]{1,0:T(8,128)S(1)}, s32[4,2]{0,1:T(2,128)S(1)}, f32[4,128,128]{2,1,0:T(8,128)}, s32[]{:T(128)}) %tuple.35), condition=%wide.while_cond, body=%wide.while_body.sunk | while | flops 2 | bytes 132705 | solution.py:60
  437.1 2.0 bitcast_dynamic-update-slice_fusion.2
  439.7 2.0 bitcast_dynamic-update-slice_fusion.2
  442.2 2.0 bitcast_dynamic-update-slice_fusion.2
  444.8 2.0 bitcast_dynamic-update-slice_fusion.2
  446.8 40.1 %custom-call.34 = f32[4,128,128]{1,2,0:T(8,128)S(1)} custom-call(f32[4,128,128]{2,1,0:T(8,128)} %get-tuple-element.9), custom_call_target="InvertDiagBlocksLowerTriangular" | custom-call | tf_op jit(solution)/shard_map/jit(_solve_triangular)/triangular_solve | solution.py:60
  488.9 1.3 fusion.22
  493.4 80.1 %all-gather.8.cloned.1.call-done = f32[512,512]{0,1:T(8,128)} async-done(((f32[512,16]{0,1:T(8,128)}), f32[512,512]{0,1:T(8,128)}) %all-gather.8.cloned.1.call-update) | async-done | bytes 1048592 | tf_op jit(solution)/shard_map/all_gather | solution.py:61
  573.5 1.7 convolution_subtract_fusion.5
  (87 shorter events, 20.6 us)
Async XLA Ops:
  7.2 139.3 %all-gather.4.cloned.1.call-start = ((), (), s32[]{:S(2)}) async-start(), calls=%async_computation.2 | async-start | bytes 6488064 | tf_op jit(solution)/shard_map/all_gather | solution.py:46
  7.2 2.1 copy-start.2
  9.3 3.2 copy-start.10
  9.9 1.9 copy-start
  11.8 134.6 %copy-start.7 = (f32[3072]{0:T(1024)S(1)}, f32[3072]{0:T(1024)}, u32[]{:S(2)}) copy-start(f32[3072]{0:T(1024)} %param.9) | copy-start | bytes 36868
  11.8 134.6 %copy-start.8 = (f32[3072]{0:T(1024)S(1)}, f32[3072]{0:T(1024)}, u32[]{:S(2)}) copy-start(f32[3072]{0:T(1024)} %param.10) | copy-start | bytes 36868
  11.8 134.6 %copy-start.9 = (s32[3072]{0:T(1024)S(1)}, s32[3072]{0:T(1024)}, u32[]{:S(2)}) copy-start(s32[3072]{0:T(1024)} %param.11) | copy-start | bytes 36868
  12.5 217.7 %reduce-scatter.2.cloned.1.call-start = ((), (), s32[]{:S(2)}) async-start(), calls=%async_computation.3 | async-start | bytes 2785280 | tf_op jit(solution)/shard_map/reduce_scatter | solution.py:48
  156.0 194.5 %all-gather.6.cloned.1.call-start = ((), (), s32[]{:S(2)}) async-start(), calls=%async_computation.4 | async-start | bytes 1081344 | tf_op jit(solution)/shard_map/all_gather | solution.py:57
  260.0 313.5 %all-gather.8.cloned.1.call-start = ((), (), s32[]{:S(2)}) async-start(), calls=%async_computation.5 | async-start | bytes 1081344 | tf_op jit(solution)/shard_map/all_gather | solution.py:61
  350.4 1.7 copy-start.1
  374.9 61.5 %copy-start.11 = (s32[4]{0:T(128)S(1)}, s32[4]{0:T(128)}, u32[]{:S(2)}) copy-start(s32[4]{0:T(128)} %iota_multiply_fusion) | copy-start | bytes 52
  375.3 111.7 %copy-start.4 = (f32[4,32,640]{2,1,0:T(8,128)S(1)}, f32[4,32,640]{2,1,0:T(8,128)}, u32[]{:S(2)}) copy-start(f32[4,32,640]{2,1,0:T(8,128)} %get-tuple-element.20) | copy-start | bytes 983044
  397.3 90.2 %copy-start.3 = (f32[4,32,640]{2,1,0:T(8,128)S(1)}, f32[4,32,640]{2,1,0:T(8,128)}, u32[]{:S(2)}) copy-start(f32[4,32,640]{2,1,0:T(8,128)} %get-tuple-element.23) | copy-start | bytes 983044
  436.3 52.1 %copy-start.5 = (f32[4,32,640]{2,1,0:T(8,128)S(1)}, f32[4,32,640]{2,1,0:T(8,128)}, u32[]{:S(2)}) copy-start(f32[4,32,640]{2,1,0:T(8,128)} %get-tuple-element.22) | copy-start | bytes 983044
  486.9 1.4 copy-start.6
Sparse Core Ops, SparseCore 0:
  12.6 105.7 all-gather.3
  156.1 74.1 reduce-scatter.1
  260.1 90.2 all-gather.5
  493.5 79.9 all-gather.7
